TPU v7x, 32 devices: a whole 2x2x4 slice. The times are simulated.
32 devices in a mesh: row: 4 (over y, x), col: 8 (over z, core).
Axes of the slice: x: 2, y: 2, z: 4, core: 2. Of those that a mesh axis runs over, the one named last changes fastest.
Arguments:
- inputs: bfloat16 [2048, 25600], P('row', 'col'), may hold values from -6 to 6
- out_grads: bfloat16 [2048, 5120], P('col', 'row'), may hold values from -0.125 to 0.125
- weights: bfloat16 [5120, 25600], P('row', 'col'), may hold values from -3 to 3
- momentum: float32 [5120, 25600], P('row', 'col'), may hold values from -13 to 13
- right_factor: float32 [25600, 256], P('col'), may hold values from -6 to 6
Outputs:
- weights_new: float32 [5120, 25600], P('row', 'col')
- momentum_new: float32 [5120, 25600], P('row', 'col')
- factor_new: float32 [25600, 256], P('col')
All inputs are finite; a program needn't handle non-finite values.
Results may differ from a plain program's by a relative error of at most 0.0003.
Values may be sent and summed in bfloat16 or wider, within the bound.
No kernel may reach another device: no remote copies, remote signals or barrier semaphores. Data moves between devices by JAX's collectives and lax.ppermute only.
A program may use at most 128 MiB of HBM per device.

v0:
```python
import math
import jax
import jax.numpy as jnp
from jax import lax
from jax.sharding import PartitionSpec as P

M = 5120
N = 25600
RANK = 256
mix_rate = 0.95
step_rate = 0.3
weight_decay = 0.1
tiny_eps = 1e-06
highest = lax.Precision.HIGHEST


def inner_rows(left_side, right_in):
    return lax.dot_general(left_side, right_in, (((0,), (0,)), ((), ())), precision=highest)


def orthonormal(sketch_rows, gram_total):
    factor_low = jnp.linalg.cholesky(gram_total)
    return jax.scipy.linalg.solve_triangular(factor_low, sketch_rows.T, lower=True).T


def on_device(inputs, out_grads, weights, momentum, right_factor):
    grads_all = lax.all_gather(out_grads, "col", axis=0, tiled=True)
    gradient = lax.dot_general(
        grads_all,
        lax.all_gather(inputs, "row", axis=0, tiled=True),
        (((0,), (0,)), ((), ())),
        preferred_element_type=jnp.float32,
    )
    moment = momentum + gradient
    sketch_part = jnp.dot(moment, right_factor, precision=highest)
    sketch_rows = lax.psum(sketch_part, "col")
    gram_total = lax.psum(inner_rows(sketch_rows, sketch_rows), "row")
    basis_rows = orthonormal(sketch_rows, gram_total)
    right_part = inner_rows(moment, basis_rows)
    right_share = lax.psum_scatter(right_part, "row", scatter_dimension=0, tiled=True)
    squares = lax.psum(jnp.sum(right_share * right_share, axis=0), ("row", "col"))
    right_side = lax.all_gather(right_share, "row", axis=0, tiled=True)
    column_scale = lax.rsqrt(squares / N + tiny_eps)
    factor_new = right_side * column_scale
    momentum_new = moment - (1.0 - mix_rate) * jnp.dot(basis_rows, right_side.T, precision=highest)
    update = jnp.dot(basis_rows, factor_new.T, precision=highest)
    weights_new = (
        weights.astype(jnp.float32) * (1.0 - step_rate * weight_decay)
        - step_rate * math.sqrt(M / RANK) * update
    )
    return (weights_new, momentum_new, factor_new)


def solution(mesh):
    placed = (P("row", "col"), P("col", "row"), P("row", "col"), P("row", "col"), P("col", None))
    return jax.shard_map(
        on_device,
        mesh=mesh,
        in_specs=placed,
        out_specs=(P("row", "col"), P("row", "col"), P("col", None)),
        check_vma=False,
    )
```

profile of v0, /device:TPU:0, one launch (start us, length us, event | category | flops | bytes accessed | tf_op | source)
XLA Modules:
  0.0 616.2 jit_solution(3706774686516627048)
XLA Ops:
  7.2 0.7 all-gather.4.cloned.1.call-update
  8.0 0.7 all-gather.6.cloned.1.call-update
  8.7 59.7 %all-gather.4.cloned.1.call-done = bf16[2048,1280]{1,0:T(8,128)(2,1)} async-done(((bf16[256,1280]{1,0:T(8,128)(2,1)}), bf16[2048,1280]{1,0:T(8,128)(2,1)}) %all-gather.4.cloned.1.call-update) | async-done | bytes 5242896 | tf_op jit(solution)/shard_map/all_gather | solution.py:27
  68.4 127.4 %all-gather.6.cloned.1.call-done = bf16[2048,3200]{1,0:T(8,128)(2,1)} async-done(((bf16[512,3200]{1,0:T(8,128)(2,1)}), bf16[2048,3200]{1,0:T(8,128)(2,1)}) %all-gather.6.cloned.1.call-update) | async-done | bytes 13107216 | tf_op jit(solution)/shard_map/all_gather | solution.py:30
  195.8 29.4 %convolution_add_fusion = f32[1280,3200]{1,0:T(8,128)} fusion(f32[1280,3200]{1,0:T(8,128)} %param.8, bf16[2048,1280]{1,0:T(8,128)(2,1)} %all-gather.4.cloned.1.call-done, bf16[2048,3200]{1,0:T(8,128)(2,1)} %all-gather.6.cloned.1.call-done), kind=kOutput, calls=%fused_computation.2 | convolution fusion | flops 16781312000 | bytes 51118080 | tf_op jit(solution)/shard_map/dot_general | solution.py:28
  225.1 17.8 %fusion.15 = f32[1280,256]{1,0:T(8,128)} fusion(f32[1280,3200]{1,0:T(8,128)} %convolution_add_fusion, f32[3200,256]{1,0:T(8,128)S(1)} %copy-done), kind=kOutput, calls=%fused_computation.41 | convolution fusion | flops 12582912000 | bytes 20971520 | tf_op jit(solution)/shard_map/dot_general | solution.py:35
  243.0 60.5 %all-reduce.4.cloned.1.call-done = f32[1280,256]{1,0:T(8,128)} async-done(((f32[1280,256]{1,0:T(8,128)}), f32[1280,256]{1,0:T(8,128)}) %all-reduce.4.cloned.1.call-update) | async-done | bytes 1310736 | tf_op jit(solution)/shard_map/psum | solution.py:36
  303.5 4.8 fusion.16
  308.6 42.0 %all-reduce.6.cloned.1.call-done = f32[256,256]{0,1:T(8,128)} async-done(((f32[256,256]{0,1:T(8,128)}), f32[256,256]{0,1:T(8,128)}) %all-reduce.6.cloned.1.call-update) | async-done | bytes 262160 | tf_op jit(solution)/shard_map/psum | solution.py:37
  350.6 1.1 copy.9
  351.7 1.0 fusion.5
  352.7 11.7 %cholesky.50 = f32[128,128]{1,0:T(8,128)S(1)} custom-call(f32[128,128]{1,0:T(8,128)S(1)} %cholesky.118), custom_call_target="Cholesky" | custom-call | tf_op jit(solution)/shard_map/jit(cholesky)/cholesky | solution.py:22
  364.4 9.8 %custom-call.15 = f32[1,128,128]{1,2,0:T(8,128)S(1)} custom-call(f32[1,128,128]{2,1,0:T(8,128)S(1)} %get-tuple-element.24), custom_call_target="InvertDiagBlocksLowerTriangular" | custom-call | tf_op jit(solution)/shard_map/jit(cholesky)/cholesky | solution.py:22
  374.8 11.7 %cholesky.105 = f32[128,128]{1,0:T(8,128)S(1)} custom-call(f32[128,128]{1,0:T(8,128)S(1)} %convolution_subtract_fusion.1), custom_call_target="Cholesky" | custom-call | tf_op jit(solution)/shard_map/jit(cholesky)/cholesky | solution.py:22
  386.5 0.7 compare_reduce_fusion
  388.6 4.2 while.1
  388.8 0.6 fusion.31
  389.4 1.4 bitcast_dynamic-update-slice_fusion.2
  390.8 0.6 fusion.31
  391.4 1.4 bitcast_dynamic-update-slice_fusion.2
  392.8 19.7 %custom-call.16 = f32[2,128,128]{1,2,0:T(8,128)S(1)} custom-call(f32[2,128,128]{2,1,0:T(8,128)S(1)} %get-tuple-element.10), custom_call_target="InvertDiagBlocksLowerTriangular" | custom-call | tf_op jit(solution)/shard_map/jit(_solve_triangular)/triangular_solve | solution.py:23
  412.5 0.8 fusion.3
  413.3 1.2 convolution_subtract_fusion
  414.5 0.8 fusion.7
  415.2 32.1 %fusion.2 = f32[3200,256]{1,0:T(8,128)} fusion(f32[1280,3200]{1,0:T(8,128)} %convolution_add_fusion, f32[128,1280]{1,0:T(8,128)S(1)} %fusion.7, f32[128,1280]{1,0:T(8,128)S(1)} %fusion.3), kind=kOutput, calls=%fused_computation.11 | convolution fusion | flops 12583239680 | bytes 20971520 | tf_op jit(solution)/shard_map/dot_general | solution.py:18
  447.4 45.1 %reduce-scatter.2.cloned.1.call-done = f32[800,256]{1,0:T(8,128)} async-done(((f32[3200,256]{1,0:T(8,128)}), f32[800,256]{1,0:T(8,128)}) %reduce-scatter.2.cloned.1.call-update) | async-done | bytes 819216 | tf_op jit(solution)/shard_map/reduce_scatter | solution.py:40
  492.6 1.3 multiply_reduce_fusion
  493.8 40.3 %psum.23 = f32[256]{0:T(256)S(1)} all-reduce(f32[256]{0:T(256)S(1)} %multiply_reduce_fusion), channel_id=1, replica_groups=mesh['row'=4,'col'=8] {'row','col'}, use_global_device_ids=true, to_apply=%region_8.9 | all-reduce | flops 256 | bytes 2048 | tf_op jit(solution)/shard_map/psum | solution.py:41
  534.1 6.0 all-gather.8.cloned.1.call-done
  540.1 2.1 broadcast_multiply_fusion
  542.3 32.8 %fusion.1 = f32[1280,3200]{1,0:T(8,128)} fusion(f32[3200,256]{1,0:T(8,128)S(1)} %broadcast_multiply_fusion, bf16[1280,3200]{1,0:T(8,128)(2,1)} %param.7, f32[128,1280]{1,0:T(8,128)S(1)} %fusion.7, f32[128,1280]{1,0:T(8,128)S(1)} %fusion.3), kind=kOutput, calls=%fused_computation.6 | convolution fusion | flops 12599623680 | bytes 29163520 | tf_op jit(solution)/shard_map/dot_general | solution.py:46
  575.0 34.1 %fusion = f32[1280,3200]{1,0:T(8,128)} fusion(f32[1280,3200]{1,0:T(8,128)} %convolution_add_fusion, f32[3200,256]{1,0:T(8,128)S(1)} %copy-done.4, f32[128,1280]{1,0:T(8,128)} %copy-done.6, f32[128,1280]{1,0:T(8,128)} %copy-done.2), kind=kOutput, calls=%fused_computation.4 | convolution fusion | flops 12591431680 | bytes 37355520 | tf_op jit(solution)/shard_map/dot_general | solution.py:45
  (37 shorter events, 1.2 us)
Async XLA Ops:
  7.2 217.9 %copy-start = (f32[3200,256]{1,0:T(8,128)S(1)}, f32[3200,256]{1,0:T(8,128)}, u32[]{:S(2)}) copy-start(f32[3200,256]{1,0:T(8,128)} %param.9) | copy-start | bytes 9830404
  7.2 61.2 %all-gather.4.cloned.1.call-start = ((), (), s32[]{:S(2)}) async-start(), calls=%async_computation.1 | async-start | bytes 5898240 | tf_op jit(solution)/shard_map/all_gather | solution.py:27
  7.9 187.8 %all-gather.6.cloned.1.call-start = ((), (), s32[]{:S(2)}) async-start(), calls=%async_computation.2 | async-start | bytes 16384000 | tf_op jit(solution)/shard_map/all_gather | solution.py:30
  8.7 294.8 %all-reduce.4.cloned.1.call-start = ((), (), s32[]{:S(2)}) async-start(), calls=%async_computation.3 | async-start | bytes 2621440 | tf_op jit(solution)/shard_map/psum | solution.py:36
  242.9 107.7 %all-reduce.6.cloned.1.call-start = ((), (), s32[]{:S(2)}) async-start(), calls=%async_computation.4 | async-start | bytes 524288 | tf_op jit(solution)/shard_map/psum | solution.py:37
  303.5 109.0 %copy-start.5 = (f32[1280,256]{1,0:T(8,128)S(1)}, f32[1280,256]{1,0:T(8,128)}, u32[]{:S(2)}) copy-start(f32[1280,256]{1,0:T(8,128)} %all-reduce.4.cloned.1.call-done) | copy-start | bytes 3932164
  308.4 184.2 %reduce-scatter.2.cloned.1.call-start = ((), (), s32[]{:S(2)}) async-start(), calls=%async_computation.5 | async-start | bytes 4096000 | tf_op jit(solution)/shard_map/reduce_scatter | solution.py:40
  413.3 129.0 %copy-start.2 = (f32[128,1280]{1,0:T(8,128)}, f32[128,1280]{1,0:T(8,128)S(1)}, u32[]{:S(2)}) copy-start(f32[128,1280]{1,0:T(8,128)S(1)} %fusion.3) | copy-start | bytes 1966084
  415.2 127.0 %copy-start.6 = (f32[128,1280]{1,0:T(8,128)}, f32[128,1280]{1,0:T(8,128)S(1)}, u32[]{:S(2)}) copy-start(f32[128,1280]{1,0:T(8,128)S(1)} %fusion.7) | copy-start | bytes 1966084
  447.4 92.7 %all-gather.8.cloned.1.call-start = ((), (), s32[]{:S(2)}) async-start(), calls=%async_computation.6 | async-start | bytes 4096000 | tf_op jit(solution)/shard_map/all_gather | solution.py:42
  542.2 32.8 %copy-start.3 = (f32[3200,256]{1,0:T(8,128)}, f32[3200,256]{1,0:T(8,128)S(1)}, u32[]{:S(2)}) copy-start(f32[3200,256]{1,0:T(8,128)S(1)} %broadcast_multiply_fusion) | copy-start | bytes 9830404
  542.3 32.8 %copy-start.4 = (f32[3200,256]{1,0:T(8,128)S(1)}, f32[3200,256]{1,0:T(8,128)}, u32[]{:S(2)}) copy-start(f32[3200,256]{1,0:T(8,128)} %all-gather.8.cloned.1.call-done) | copy-start | bytes 9830404
  575.0 34.1 %copy-start.1 = (f32[3200,256]{1,0:T(8,128)S(1)}, f32[3200,256]{1,0:T(8,128)}, u32[]{:S(2)}) copy-start(f32[3200,256]{1,0:T(8,128)} %param.9) | copy-start | bytes 9830404
Sparse Core Ops, SparseCore 0:
  9.6 58.6 all-gather.3
  70.2 125.5 all-gather.5
  243.0 60.4 all-reduce.3
  308.5 42.0 all-reduce.5
  447.5 44.9 reduce-scatter.1
  494.2 45.7 all-gather.7
where the time goes:
time: 623 us; the launch traced here: 616 us
  waiting for transfers between devices  342 us (55%)
  matrix products  154 us (25%)
  other arithmetic  58.1 us (9%)
  blocking collectives  40.3 us (6%)
  between operations  15.8 us (3%)
    all_gather x1, waiting for transfers between devices, on_device(): lax.all_gather(inputs, 'row', axis=0, tiled=True)  127 us
    psum x1, waiting for transfers between devices, on_device(): sketch_rows = lax.psum(sketch_part, 'col')  60.5 us
    all_gather x1, waiting for transfers between devices, on_device(): grads_all = lax.all_gather(out_grads, 'col', axis=0, tiled=True)  59.7 us
    reduce_scatter x1, waiting for transfers between devices, on_device(): lax.psum_scatter(right_part, 'row', scatter_dimension=0, tiled=True)  45.1 us
    psum x1, waiting for transfers between devices, on_device(): gram_total = lax.psum(inner_rows(sketch_rows, sketch_rows), 'row')  42 us
    psum x1, blocking collectives, on_device(): lax.psum(jnp.sum(right_share * right_share, axis=0), ('row', 'col'))  40.3 us
    dot_general x2, matrix products, inner_rows(): lax.dot_general(left_side, right_in, (((0,), (0,)), ((), ())), precision=...  36.9 us
    dot_general x1, matrix products, on_device(): jnp.dot(basis_rows, right_side.T, precision=highest)  34.1 us
  transfers between devices with their start and end apart: 6, of which 6 were waited for; matrix products, arithmetic and copies ran while one was open for 0% of the time, Pallas kernels for 0%

commit v1 on v0

--- a/solution.py
+++ b/solution.py
@@ -33,7 +33,11 @@
     )
     moment = momentum + gradient
     sketch_part = jnp.dot(moment, right_factor, precision=highest)
-    sketch_rows = lax.psum(sketch_part, "col")
+    sketch_rows = sketch_part
+    for hop in (1, 2, 4):
+        sketch_rows = sketch_rows + lax.ppermute(
+            sketch_rows, "col", [(dev, dev ^ hop) for dev in range(8)]
+        )
     gram_total = lax.psum(inner_rows(sketch_rows, sketch_rows), "row")
     basis_rows = orthonormal(sketch_rows, gram_total)
     right_part = inner_rows(moment, basis_rows)

time: 623 us -> 653 us (1.048)
  waiting for transfers between devices: 342 us -> 370 us
    ppermute x0 -> x3, waiting for transfers between devices: none -> 88.9 us  [on_device(): lax.ppermute(sketch_rows, 'col', [(dev, dev ^ hop) for dev in range(8)])]
    psum x1 -> x0, waiting for transfers between devices: 60.5 us -> none  [on_device(): sketch_rows = lax.psum(sketch_part, 'col')]
  transfers between devices with their start and end apart: 6 -> 8, of which waited for: 6 -> 8; matrix products, arithmetic and copies ran while one was open for 0% -> 0% of each run, Pallas kernels for 0% -> 0%
where the time goes in v1:
time: 653 us; the launch traced here: 646 us
  waiting for transfers between devices  370 us (57%)
  matrix products  151 us (23%)
  other arithmetic  59.9 us (9%)
  blocking collectives  40.2 us (6%)
  between operations  15.7 us (2%)
    all_gather x1, waiting for transfers between devices, on_device(): lax.all_gather(inputs, 'row', axis=0, tiled=True)  127 us
    ppermute x3, waiting for transfers between devices, on_device(): lax.ppermute(sketch_rows, 'col', [(dev, dev ^ hop) for dev in range(8)])  88.9 us
    all_gather x1, waiting for transfers between devices, on_device(): grads_all = lax.all_gather(out_grads, 'col', axis=0, tiled=True)  59.7 us
    reduce_scatter x1, waiting for transfers between devices, on_device(): lax.psum_scatter(right_part, 'row', scatter_dimension=0, tiled=True)  45.1 us
    psum x1, waiting for transfers between devices, on_device(): gram_total = lax.psum(inner_rows(sketch_rows, sketch_rows), 'row')  41.2 us
    psum x1, blocking collectives, on_device(): lax.psum(jnp.sum(right_share * right_share, axis=0), ('row', 'col'))  40.2 us
    dot_general x2, matrix products, inner_rows(): lax.dot_general(left_side, right_in, (((0,), (0,)), ((), ())), precision=...  34.8 us
    another operation x6, other arithmetic, orthonormal(): factor_low = jnp.linalg.cholesky(gram_total)  34 us
  transfers between devices with their start and end apart: 8, of which 8 were waited for; matrix products, arithmetic and copies ran while one was open for 0% of the time, Pallas kernels for 0%

profile of v1, /device:TPU:0, one launch (start us, length us, event | category | flops | bytes accessed | tf_op | source)
XLA Modules:
  0.0 646.2 jit_solution(17672954261898459536)
XLA Ops:
  8.7 59.7 %all-gather.4.cloned.1.call-done = bf16[2048,1280]{1,0:T(8,128)(2,1)} async-done(((bf16[256,1280]{1,0:T(8,128)(2,1)}), bf16[2048,1280]{1,0:T(8,128)(2,1)}) %all-gather.4.cloned.1.call-update) | async-done | bytes 5242896 | tf_op jit(solution)/shard_map/all_gather | solution.py:27
  68.4 127.4 %all-gather.6.cloned.1.call-done = bf16[2048,3200]{1,0:T(8,128)(2,1)} async-done(((bf16[512,3200]{1,0:T(8,128)(2,1)}), bf16[2048,3200]{1,0:T(8,128)(2,1)}) %all-gather.6.cloned.1.call-update) | async-done | bytes 13107216 | tf_op jit(solution)/shard_map/all_gather | solution.py:30
  195.8 29.4 %convolution_add_fusion = f32[1280,3200]{1,0:T(8,128)} fusion(f32[1280,3200]{1,0:T(8,128)} %param.8, bf16[2048,1280]{1,0:T(8,128)(2,1)} %all-gather.4.cloned.1.call-done, bf16[2048,3200]{1,0:T(8,128)(2,1)} %all-gather.6.cloned.1.call-done), kind=kOutput, calls=%fused_computation.2 | convolution fusion | flops 16781312000 | bytes 51118080 | tf_op jit(solution)/shard_map/dot_general | solution.py:28
  225.1 16.8 %fusion.18 = f32[1280,256]{1,0:T(8,128)S(1)} fusion(f32[1280,3200]{1,0:T(8,128)} %convolution_add_fusion, f32[3200,256]{1,0:T(8,128)S(1)} %copy-done), kind=kOutput, calls=%fused_computation.45 | convolution fusion | flops 12582912000 | bytes 20971520 | tf_op jit(solution)/shard_map/dot_general | solution.py:35
  242.0 3.0 collective-permute-done
  245.2 1.6 collective-permute-start.1
  246.8 29.3 %collective-permute-done.1 = f32[1280,256]{1,0:T(8,128)S(1)} collective-permute-done((f32[1280,256]{1,0:T(8,128)S(1)}, f32[1280,256]{1,0:T(8,128)S(1)}, u32[]{:S(2)}, u32[]{:S(2)}) %collective-permute-start.1) | collective-permute-done | bytes 1310752 | tf_op jit(solution)/shard_map/ppermute | solution.py:38
  276.3 2.5 collective-permute-start.2
  278.7 56.5 %collective-permute-done.2 = f32[1280,256]{1,0:T(8,128)S(1)} collective-permute-done((f32[1280,256]{1,0:T(8,128)S(1)}, f32[1280,256]{1,0:T(8,128)S(1)}, u32[]{:S(2)}, u32[]{:S(2)}) %collective-permute-start.2) | collective-permute-done | bytes 1310752 | tf_op jit(solution)/shard_map/ppermute | solution.py:38
  335.3 3.0 fusion.6
  338.8 1.5 add_bitcast_fusion
  340.2 41.2 %all-reduce.3.cloned.1.call-done = f32[256,256]{0,1:T(8,128)} async-done(((f32[256,256]{0,1:T(8,128)}), f32[256,256]{0,1:T(8,128)}) %all-reduce.3.cloned.1.call-update) | async-done | bytes 262160 | tf_op jit(solution)/shard_map/psum | solution.py:41
  381.5 1.1 copy.9
  382.6 1.0 fusion.8
  383.6 11.7 %cholesky.50 = f32[128,128]{1,0:T(8,128)S(1)} custom-call(f32[128,128]{1,0:T(8,128)S(1)} %cholesky.118), custom_call_target="Cholesky" | custom-call | tf_op jit(solution)/shard_map/jit(cholesky)/cholesky | solution.py:22
  395.3 9.8 %custom-call.15 = f32[1,128,128]{1,2,0:T(8,128)S(1)} custom-call(f32[1,128,128]{2,1,0:T(8,128)S(1)} %get-tuple-element.24), custom_call_target="InvertDiagBlocksLowerTriangular" | custom-call | tf_op jit(solution)/shard_map/jit(cholesky)/cholesky | solution.py:22
  405.6 11.7 %cholesky.105 = f32[128,128]{1,0:T(8,128)S(1)} custom-call(f32[128,128]{1,0:T(8,128)S(1)} %convolution_subtract_fusion), custom_call_target="Cholesky" | custom-call | tf_op jit(solution)/shard_map/jit(cholesky)/cholesky | solution.py:22
  419.4 4.0 while.1
  420.0 1.4 bitcast_dynamic-update-slice_fusion.2
  422.0 1.4 bitcast_dynamic-update-slice_fusion.2
  423.4 19.7 %custom-call.16 = f32[2,128,128]{1,2,0:T(8,128)S(1)} custom-call(f32[2,128,128]{2,1,0:T(8,128)S(1)} %get-tuple-element.10), custom_call_target="InvertDiagBlocksLowerTriangular" | custom-call | tf_op jit(solution)/shard_map/jit(_solve_triangular)/triangular_solve | solution.py:23
  443.1 0.8 fusion.4
  443.9 1.2 fusion.9
  445.1 0.7 fusion.3
  445.8 31.8 %fusion.2 = f32[3200,256]{1,0:T(8,128)} fusion(f32[1280,3200]{1,0:T(8,128)} %convolution_add_fusion, f32[128,1280]{1,0:T(8,128)S(1)} %fusion.3, f32[128,1280]{1,0:T(8,128)S(1)} %fusion.4), kind=kOutput, calls=%fused_computation.10 | convolution fusion | flops 12583239680 | bytes 20971520 | tf_op jit(solution)/shard_map/dot_general | solution.py:18
  477.8 45.1 %reduce-scatter.2.cloned.1.call-done = f32[800,256]{1,0:T(8,128)} async-done(((f32[3200,256]{1,0:T(8,128)}), f32[800,256]{1,0:T(8,128)}) %reduce-scatter.2.cloned.1.call-update) | async-done | bytes 819216 | tf_op jit(solution)/shard_map/reduce_scatter | solution.py:44
  522.9 1.3 multiply_reduce_fusion
  524.2 40.2 %psum.15 = f32[256]{0:T(256)S(1)} all-reduce(f32[256]{0:T(256)S(1)} %multiply_reduce_fusion), channel_id=1, replica_groups=mesh['row'=4,'col'=8] {'row','col'}, use_global_device_ids=true, to_apply=%region_7.8 | all-reduce | flops 256 | bytes 2048 | tf_op jit(solution)/shard_map/psum | solution.py:45
  564.4 6.0 all-gather.8.cloned.1.call-done
  570.4 2.1 broadcast_multiply_fusion
  572.6 32.8 %fusion.1 = f32[1280,3200]{1,0:T(8,128)} fusion(f32[3200,256]{1,0:T(8,128)S(1)} %broadcast_multiply_fusion, bf16[1280,3200]{1,0:T(8,128)(2,1)} %param.7, f32[128,1280]{1,0:T(8,128)S(1)} %fusion.3, f32[128,1280]{1,0:T(8,128)S(1)} %fusion.4), kind=kOutput, calls=%fused_computation.6 | convolution fusion | flops 12599623680 | bytes 29163520 | tf_op jit(solution)/shard_map/dot_general | solution.py:50
  605.4 33.9 %fusion = f32[1280,3200]{1,0:T(8,128)} fusion(f32[1280,3200]{1,0:T(8,128)} %convolution_add_fusion, f32[3200,256]{1,0:T(8,128)S(1)} %copy-done.4, f32[128,1280]{1,0:T(8,128)} %copy-done.5, f32[128,1280]{1,0:T(8,128)} %copy-done.2), kind=kOutput, calls=%fused_computation.4 | convolution fusion | flops 12591431680 | bytes 37355520 | tf_op jit(solution)/shard_map/dot_general | solution.py:49
  (43 shorter events, 5.0 us)
Async XLA Ops:
  7.2 217.9 %copy-start = (f32[3200,256]{1,0:T(8,128)S(1)}, f32[3200,256]{1,0:T(8,128)}, u32[]{:S(2)}) copy-start(f32[3200,256]{1,0:T(8,128)} %param.9) | copy-start | bytes 9830404
  7.2 61.2 %all-gather.4.cloned.1.call-start = ((), (), s32[]{:S(2)}) async-start(), calls=%async_computation.1 | async-start | bytes 5898240 | tf_op jit(solution)/shard_map/all_gather | solution.py:27
  7.9 187.8 %all-gather.6.cloned.1.call-start = ((), (), s32[]{:S(2)}) async-start(), calls=%async_computation.2 | async-start | bytes 16384000 | tf_op jit(solution)/shard_map/all_gather | solution.py:30
  8.7 372.8 %all-reduce.3.cloned.1.call-start = ((), (), s32[]{:S(2)}) async-start(), calls=%async_computation.3 | async-start | bytes 524288 | tf_op jit(solution)/shard_map/psum | solution.py:41
  241.9 3.1 collective-permute-start
  245.2 30.9 %collective-permute-start.1 = (f32[1280,256]{1,0:T(8,128)S(1)}, f32[1280,256]{1,0:T(8,128)S(1)}, u32[]{:S(2)}, u32[]{:S(2)}) collective-permute-start(f32[1280,256]{1,0:T(8,128)S(1)} %add.48), channel_id=1, source_target_pairs={{0,2},{1,3},{2,0},{3,1},{4,6},{5,7},{6,4},{7,5},{8,10},{9,11},{10,... | collective-permute-start | bytes 3932168 | tf_op jit(solution)/shard_map/ppermute | solution.py:38
  276.3 59.0 %collective-permute-start.2 = (f32[1280,256]{1,0:T(8,128)S(1)}, f32[1280,256]{1,0:T(8,128)S(1)}, u32[]{:S(2)}, u32[]{:S(2)}) collective-permute-start(f32[1280,256]{1,0:T(8,128)S(1)} %add.49), channel_id=1, source_target_pairs={{0,4},{1,5},{2,6},{3,7},{4,0},{5,1},{6,2},{7,3},{8,12},{9,13},{10,... | collective-permute-start | bytes 3932168 | tf_op jit(solution)/shard_map/ppermute | solution.py:38
  335.3 3.0 copy-start.6
  338.3 184.6 %reduce-scatter.2.cloned.1.call-start = ((), (), s32[]{:S(2)}) async-start(), calls=%async_computation.4 | async-start | bytes 4096000 | tf_op jit(solution)/shard_map/reduce_scatter | solution.py:44
  443.9 128.7 %copy-start.2 = (f32[128,1280]{1,0:T(8,128)}, f32[128,1280]{1,0:T(8,128)S(1)}, u32[]{:S(2)}) copy-start(f32[128,1280]{1,0:T(8,128)S(1)} %fusion.4) | copy-start | bytes 1966084
  445.8 126.7 %copy-start.5 = (f32[128,1280]{1,0:T(8,128)}, f32[128,1280]{1,0:T(8,128)S(1)}, u32[]{:S(2)}) copy-start(f32[128,1280]{1,0:T(8,128)S(1)} %fusion.3) | copy-start | bytes 1966084
  477.7 92.7 %all-gather.8.cloned.1.call-start = ((), (), s32[]{:S(2)}) async-start(), calls=%async_computation.5 | async-start | bytes 4096000 | tf_op jit(solution)/shard_map/all_gather | solution.py:46
  572.6 32.8 %copy-start.3 = (f32[3200,256]{1,0:T(8,128)}, f32[3200,256]{1,0:T(8,128)S(1)}, u32[]{:S(2)}) copy-start(f32[3200,256]{1,0:T(8,128)S(1)} %broadcast_multiply_fusion) | copy-start | bytes 9830404
  572.6 32.8 %copy-start.4 = (f32[3200,256]{1,0:T(8,128)S(1)}, f32[3200,256]{1,0:T(8,128)}, u32[]{:S(2)}) copy-start(f32[3200,256]{1,0:T(8,128)} %all-gather.8.cloned.1.call-done) | copy-start | bytes 9830404
  605.3 33.9 %copy-start.1 = (f32[3200,256]{1,0:T(8,128)S(1)}, f32[3200,256]{1,0:T(8,128)}, u32[]{:S(2)}) copy-start(f32[3200,256]{1,0:T(8,128)} %param.9) | copy-start | bytes 9830404
Sparse Core Ops, SparseCore 0:
  9.6 58.6 all-gather.3
  70.2 125.5 all-gather.5
  338.4 43.0 all-reduce.2
  477.8 44.9 reduce-scatter.1
  524.6 45.7 all-gather.7
